TPU v7x, 32 devices: a whole 2x2x4 slice. The times are simulated.
32 devices in a mesh: con: 16 (over z, y, x), rep: 2 (over core).
Axes of the slice: x: 2, y: 2, z: 4, core: 2. Of those that a mesh axis runs over, the one named last changes fastest.
Arguments:
- tamps: bfloat16 [16384, 14336], P('rep', 'con'), may hold values from -6 to 6
- integrals: bfloat16 [1024, 16384], P('con', 'rep'), may hold values from -0.0625 to 0.0625
Outputs:
- ladder: bfloat16 [1024, 14336], P('rep', 'con')
All inputs are finite; a program needn't handle non-finite values.
Results may differ from a plain program's by a relative error of at most 0.001.
Values may be sent and summed in bfloat16 or wider, within the bound.
A program may use at most 128 MiB of HBM per device.

v0:
```python
import jax
import jax.numpy as jnp
from jax import lax
from jax.sharding import PartitionSpec as P


def shards(tamps, integrals):
    gathered = lax.all_gather(integrals, "con", axis=0, tiled=True)
    partial_value = jnp.dot(gathered, tamps, preferred_element_type=jnp.float32)
    summed = lax.psum_scatter(partial_value, "rep", scatter_dimension=0, tiled=True)
    return summed.astype(jnp.bfloat16)


def solution(mesh):
    in_specs = (P("rep", "con"), P("con", "rep"))
    out_specs = P("rep", "con")
    return jax.shard_map(shards, mesh=mesh, in_specs=in_specs, out_specs=out_specs, check_vma=False)
```

profile of v0, /device:TPU:0, one launch (start us, length us, event | category | flops | bytes accessed | tf_op | source)
XLA Modules:
  0.0 246.8 jit_solution(9029354542625471517)
XLA Ops:
  6.5 0.0 all-gather.2.cloned.1.call-start
  6.5 0.7 all-gather.2.cloned.1.call-update
  7.3 0.0 reduce-scatter.2.cloned.1.call-start
  7.3 197.2 %all-gather.2.cloned.1.call-done = bf16[1024,8192]{1,0:T(8,128)(2,1)} async-done(((bf16[64,8192]{1,0:T(8,128)(2,1)}), bf16[1024,8192]{1,0:T(8,128)(2,1)}) %all-gather.2.cloned.1.call-update) | async-done | bytes 16777232 | tf_op jit(solution)/shard_map/all_gather | solution.py:8
  204.5 23.1 %fusion = f32[1024,896]{1,0:T(8,128)} fusion(bf16[1024,8192]{1,0:T(8,128)(2,1)} %all-gather.2.cloned.1.call-done, bf16[8192,896]{1,0:T(8,128)(2,1)} %param.2), kind=kOutput, calls=%fused_computation | convolution fusion | flops 15032385536 | bytes 35127296 | tf_op jit(solution)/shard_map/dot_general | solution.py:9
  227.6 0.0 reduce-scatter.2.cloned.1.call-update
  227.6 9.9 %reduce-scatter.2.cloned.1.call-done = f32[512,896]{1,0:T(8,128)} async-done(((f32[1024,896]{1,0:T(8,128)}), f32[512,896]{1,0:T(8,128)}) %reduce-scatter.2.cloned.1.call-update) | async-done | bytes 1835024 | tf_op jit(solution)/shard_map/reduce_scatter | solution.py:10
  237.5 2.5 %convert_element_type.3 = bf16[512,896]{1,0:T(8,128)(2,1)} convert(f32[512,896]{1,0:T(8,128)} %reduce-scatter.2.cloned.1.call-done) | non-fusion elementwise | flops 458752 | bytes 2752512 | tf_op jit(solution)/shard_map/convert_element_type | solution.py:11
Async XLA Ops:
  6.5 197.9 %all-gather.2.cloned.1.call-start = ((), (), s32[]{:S(2)}) async-start(), calls=%async_computation.1 | async-start | bytes 17825792 | tf_op jit(solution)/shard_map/all_gather | solution.py:8
  7.3 230.2 %reduce-scatter.2.cloned.1.call-start = ((), (), s32[]{:S(2)}) async-start(), calls=%async_computation.2 | async-start | bytes 5505024 | tf_op jit(solution)/shard_map/reduce_scatter | solution.py:10
Sparse Core Ops, SparseCore 0:
  10.1 194.3 all-gather.1
  227.7 9.7 reduce-scatter.1
where the time goes:
time: 247 us
  waiting for transfers between devices  208 us (84%)
  matrix products  23.1 us (9%)
  between operations  13.4 us (5%)
  other arithmetic  2.52 us (1%)
    all_gather x1, waiting for transfers between devices, shards(): gathered = lax.all_gather(integrals, 'con', axis=0, tiled=True)  197 us
    dot_general x1, matrix products, shards(): partial_value = jnp.dot(gathered, tamps, preferred_element_type=jnp.float32)  23.1 us
    reduce_scatter x1, waiting for transfers between devices, shards(): lax.psum_scatter(partial_value, 'rep', scatter_dimension=0, tiled=True)  9.87 us
  transfers between devices with their start and end apart: 2, of which 2 were waited for; matrix products, arithmetic and copies ran while one was open for 0% of the time, Pallas kernels for 0%

commit v1 on v0

v1 whole, which is shorter than its diff:
```python
import functools

import jax
import jax.numpy as jnp
from jax import lax
from jax.experimental import pallas as pl
from jax.experimental.pallas import tpu as pltpu
from jax.sharding import PartitionSpec as P

MESH = pl.DeviceIdType.MESH
CHUNKS = 8
SLOTS = 40
LAG = 2
X, Y, UP, DOWN = range(4)


def plane_at(z, i):
    near = z + 1 - 2 * (z % 2)
    second = jnp.where(z < 2, 2, 1)
    third = jnp.where(z < 2, 3, 0)
    return jnp.where(i == 0, near, jnp.where(i == 1, second, third))


def message(way, t, x, y, z):
    own = y * 2 + x
    diagonal = (1 - y) * 2 + (1 - x)
    if way in (X, Y):
        side = (1 - y) * 2 + x if way == X else y * 2 + (1 - x)
        i = (t - 12) // 8
        q = t - 36
        if way == X:
            last_i = jnp.where(q == 0, 0, jnp.where(q == 3, 2, 1))
            last_c = jnp.where(q == 0, 6, jnp.where(q == 1, 5, jnp.where(q == 2, 7, 6)))
            ok = jnp.logical_or(t != 37, jnp.logical_or(z == 0, z == 3))
        else:
            last_i = jnp.where(q == 0, 0, jnp.where(q == 1, 1, 2))
            last_c = jnp.where(q == 0, 7, jnp.where(q == 1, 6, jnp.where(q == 2, 5, 7)))
            ok = t >= 0
        column = jnp.where(t < 8, own, jnp.where(t < 12, side, jnp.where(t < 36, own, side)))
        plane = jnp.where(t < 12, z, jnp.where(t < 36, plane_at(z, i), plane_at(z, last_i)))
        chunk = jnp.where(
            t < 8, t, jnp.where(t < 12, 2 * (t - 8) + way, jnp.where(t < 36, (t - 12) % 8, last_c))
        )
        return column, plane, chunk, ok
    far = jnp.where(t < 24, t // 8, jnp.where(t < 30, 0, jnp.where(t < 35, 1, 2)))
    chunk = jnp.where(t < 24, t % 8, jnp.where(t < 30, t - 24, jnp.where(t < 35, t - 30, t - 35)))
    column = jnp.where(t < 24, own, diagonal)
    if way == UP:
        plane = z - far
        ok = jnp.logical_and(jnp.logical_and(z >= 0, z < 3), plane >= 0)
    else:
        plane = z + far
        ok = jnp.logical_and(jnp.logical_and(z <= 3, z > 0), plane <= 3)
    return column, plane, chunk, ok


def units_ready(s):
    early = jnp.clip(s - 15, 0, 8) + 2 * jnp.clip(s - 27, 0, 8)
    late = jnp.clip(s - 34, 0, 4) + jnp.where(s >= 38, 1, 0) + jnp.where(s >= 39, 3, 0)
    return early + late


def kernel(
    tamps_hbm, slab_hbm, out_ref, held, amps, total, other,
    send_sem, recv_sem, own_sem, amps_sem, part_send, part_recv,
):
    me = lax.axis_index("con")
    core = lax.axis_index("rep")
    z, y, x = me // 4, (me // 2) % 2, me % 2
    rows = slab_hbm.shape[0]
    wide = slab_hbm.shape[1] // CHUNKS
    half = 2 * rows
    columns = amps.shape[1]
    own = y * 2 + x

    def device(x, y, z):
        return z * 4 + y * 2 + x

    def place(column, plane, chunk):
        start = pl.multiple_of((column * 4 + plane) * rows, rows)
        return held.at[chunk, pl.ds(start, rows), :]

    load_amps = pltpu.make_async_copy(tamps_hbm, amps, amps_sem)
    loads = [
        pltpu.make_async_copy(
            slab_hbm.at[:, pl.ds(c * wide, wide)], place(own, z, c), own_sem.at[c]
        )
        for c in range(CHUNKS)
    ]
    for load in loads:
        load.start()

    barrier = pltpu.get_barrier_semaphore()
    side = (device(1 - x, y, z), device(x, 1 - y, z))
    for to in side:
        pl.semaphore_signal(barrier, inc=1, device_id=(to, core), device_id_type=MESH)
    pl.semaphore_signal(barrier, inc=1, device_id=(me, 1 - core), device_id_type=MESH)

    @pl.when(z > 0)
    def _():
        pl.semaphore_signal(barrier, inc=1, device_id=(me - 4, core), device_id_type=MESH)

    @pl.when(z < 3)
    def _():
        pl.semaphore_signal(barrier, inc=1, device_id=(me + 4, core), device_id_type=MESH)

    ends = jnp.logical_or(z == 0, z == 3)
    pl.semaphore_wait(barrier, jnp.where(ends, 4, 5))

    for load in loads:
        load.wait()

    targets = (side[0], side[1], me + 4, me - 4)
    sources = ((1 - x, y, z), (x, 1 - y, z), (x, y, z - 1), (x, y, z + 1))

    def copy(way, t, piece):
        return pltpu.make_async_remote_copy(
            src_ref=piece,
            dst_ref=piece,
            send_sem=send_sem.at[way, t],
            recv_sem=recv_sem.at[way, t],
            device_id=(targets[way], core),
            device_id_type=MESH,
        )

    def send(t):
        for way in range(4):
            column, plane, chunk, ok = message(way, t, x, y, z)

            @pl.when(ok)
            def _():
                copy(way, t, place(column, plane, chunk)).start()

    def arrive(t):
        for way in range(4):
            column, plane, chunk, ok = message(way, t, *sources[way])

            @pl.when(ok)
            def _():
                copy(way, t, place(column, plane, chunk)).wait_recv()

    def product(u):
        m = u - 24
        pair = u - 8
        column = jnp.where(
            u < 8,
            own,
            jnp.where(
                u < 24,
                jnp.where(pair % 2 == 0, y * 2 + 1 - x, (1 - y) * 2 + x),
                (1 - y) * 2 + 1 - x,
            ),
        )
        late = jnp.where(m == 4, 5, jnp.where(m == 5, 4, m))
        chunk = jnp.where(u < 8, u, jnp.where(u < 24, pair // 2, late))
        left = held[chunk, pl.ds(pl.multiple_of(column * 4 * rows, 4 * rows), 4 * rows), :]
        deep = pl.ds(pl.multiple_of(chunk * wide, wide), wide)
        for first in range(0, columns, 256):
            cut = slice(first, min(first + 256, columns))
            total[column, :, cut] += jnp.dot(
                left, amps[deep, cut], preferred_element_type=jnp.float32
            )

    def hand_over(column):
        return pltpu.make_async_remote_copy(
            src_ref=total.at[column, pl.ds(pl.multiple_of((1 - core) * half, half), half), :],
            dst_ref=other.at[column],
            send_sem=part_send.at[column],
            recv_sem=part_recv.at[column],
            device_id=(me, 1 - core),
            device_id_type=MESH,
        )

    def step(t, _):
        @pl.when(t >= LAG)
        def _():
            arrive(t - LAG)

        @pl.when(t < SLOTS)
        def _():
            send(t)

        @pl.when(t == 8)
        def _():
            load_amps.start()
            total[...] = jnp.zeros_like(total)

        @pl.when(t == 16)
        def _():
            load_amps.wait()

        def unit(u, _):
            product(u)
            return 0

        lax.fori_loop(units_ready(t - LAG - 1), units_ready(t - LAG), unit, 0)

        @pl.when(t == 35 + LAG)
        def _():
            for column in (own, y * 2 + 1 - x, (1 - y) * 2 + x):
                hand_over(column).start()

        return 0

    lax.fori_loop(0, SLOTS + LAG, step, 0)
    hand_over((1 - y) * 2 + 1 - x).start()

    def drain(t, _):
        for way in range(4):
            column, plane, chunk, ok = message(way, t, x, y, z)

            @pl.when(ok)
            def _():
                copy(way, t, place(column, plane, chunk)).wait_send()

        return 0

    lax.fori_loop(0, SLOTS, drain, 0)

    def finish(column):
        hand_over(column).wait()
        mine = total[column, pl.ds(pl.multiple_of(core * half, half), half), :] + other[column]
        for k in range(2):
            start = pl.multiple_of((k * 4 + column) * rows, rows)
            out_ref[pl.ds(start, rows), :] = mine[k * rows : (k + 1) * rows].astype(out_ref.dtype)

    for column in (own, y * 2 + 1 - x, (1 - y) * 2 + x, (1 - y) * 2 + 1 - x):
        finish(column)


def linked(tamps, integrals):
    rows, depth = integrals.shape
    columns = tamps.shape[1]
    return pl.pallas_call(
        kernel,
        out_shape=jax.ShapeDtypeStruct((8 * rows, columns), jnp.bfloat16),
        in_specs=[pl.BlockSpec(memory_space=pl.ANY)] * 2,
        out_specs=pl.BlockSpec(memory_space=pltpu.VMEM),
        scratch_shapes=[
            pltpu.VMEM((CHUNKS, 16 * rows, depth // CHUNKS), jnp.bfloat16),
            pltpu.VMEM((depth, columns), jnp.bfloat16),
            pltpu.VMEM((4, 4 * rows, columns), jnp.float32),
            pltpu.VMEM((4, 2 * rows, columns), jnp.float32),
            pltpu.SemaphoreType.DMA((4, SLOTS)),
            pltpu.SemaphoreType.DMA((4, SLOTS)),
            pltpu.SemaphoreType.DMA((CHUNKS,)),
            pltpu.SemaphoreType.DMA,
            pltpu.SemaphoreType.DMA((4,)),
            pltpu.SemaphoreType.DMA((4,)),
        ],
        compiler_params=pltpu.CompilerParams(
            collective_id=0, has_side_effects=True, vmem_limit_bytes=56 * 2**20
        ),
    )(tamps, integrals)


def shards(tamps, integrals):
    gathered = lax.all_gather(integrals, "con", axis=0, tiled=True)
    partial_value = jnp.dot(gathered, tamps, preferred_element_type=jnp.float32)
    summed = lax.psum_scatter(partial_value, "rep", scatter_dimension=0, tiled=True)
    return summed.astype(jnp.bfloat16)


def solution(mesh):
    in_specs = (P("rep", "con"), P("con", "rep"))
    out_specs = P("rep", "con")
    part = linked if (mesh.shape["con"], mesh.shape["rep"]) == (16, 2) else shards
    return jax.shard_map(part, mesh=mesh, in_specs=in_specs, out_specs=out_specs, check_vma=False)
```

time: 247 us -> 128 us (0.52)
  waiting for transfers between devices: 208 us -> 0 us
  Pallas kernels: 0 us -> 126 us
  matrix products: 23.1 us -> 0 us
  between operations: 13.4 us -> 0.01 us
  other arithmetic: 2.52 us -> 0 us
    all_gather x1 -> x0, waiting for transfers between devices: 197 us -> none  [shards(): gathered = lax.all_gather(integrals, 'con', axis=0, tiled=True)]
    pallas_call x0 -> x1, Pallas kernels: none -> 126 us  [linked(): pl.pallas_call(kernel, out_shape=jax.ShapeDtypeStruct((8 * rows, columns)...]
    dot_general x1 -> x0, matrix products: 23.1 us -> none  [shards(): partial_value = jnp.dot(gathered, tamps, preferred_element_type=jnp.float32)]
    reduce_scatter x1 -> x0, waiting for transfers between devices: 9.87 us -> none  [shards(): lax.psum_scatter(partial_value, 'rep', scatter_dimension=0, tiled=True)]
    convert_element_type x1 -> x0, other arithmetic: 2.52 us -> none  [shards(): return summed.astype(jnp.bfloat16)]
  transfers between devices with their start and end apart: 2 -> 0, of which waited for: 2 -> 0; matrix products, arithmetic and copies ran while one was open for 0% -> 0% of each run, Pallas kernels for 0% -> 0%
where the time goes in v1:
time: 128 us
  Pallas kernels  126 us (98%)
  local copies, waits for them, and re-layouts  2.18 us (2%)
    pallas_call x1, Pallas kernels, linked(): pl.pallas_call(kernel, out_shape=jax.ShapeDtypeStruct((8 * rows, columns)...  126 us

profile of v1, /device:TPU:0, one launch (start us, length us, event | category | flops | bytes accessed | tf_op | source)
XLA Modules:
  0.0 127.7 jit_solution(4735693497799026160)
XLA Ops:
  0.0 125.5 %shard_map.28 = bf16[512,896]{1,0:T(8,128)(2,1)} custom-call(bf16[8192,896]{1,0:T(8,128)(2,1)} %tamps_hbm.1, bf16[64,8192]{1,0:T(8,128)(2,1)} %slab_hbm.1), custom_call_target="tpu_custom_call" | custom-call | tf_op jit(solution)/shard_map/pallas_call | solution.py:234
  125.5 2.2 %copy.4 = bf16[512,896]{1,0:T(8,128)(2,1)} copy(bf16[512,896]{1,0:T(8,128)(2,1)} %shard_map.28) | data formatting | bytes 1835008

commit v2 on v1

--- a/solution.py
+++ b/solution.py
@@ -10,7 +10,7 @@
 MESH = pl.DeviceIdType.MESH
 CHUNKS = 8
 SLOTS = 40
-LAG = 2
+LAG = 4
 X, Y, UP, DOWN = range(4)
 
 
@@ -19,6 +19,10 @@
     second = jnp.where(z < 2, 2, 1)
     third = jnp.where(z < 2, 3, 0)
     return jnp.where(i == 0, near, jnp.where(i == 1, second, third))
+
+
+def turned(n):
+    return jnp.where(n < 16, n, n + 5) % 8
 
 
 def message(way, t, x, y, z):
@@ -29,34 +33,42 @@
         i = (t - 12) // 8
         q = t - 36
         if way == X:
-            last_i = jnp.where(q == 0, 0, jnp.where(q == 3, 2, 1))
-            last_c = jnp.where(q == 0, 6, jnp.where(q == 1, 5, jnp.where(q == 2, 7, 6)))
-            ok = jnp.logical_or(t != 37, jnp.logical_or(z == 0, z == 3))
+            last_i = jnp.where(q == 1, 0, 1)
+            last_c = jnp.where(q == 0, 6, jnp.where(q == 3, 4, 7))
         else:
-            last_i = jnp.where(q == 0, 0, jnp.where(q == 1, 1, 2))
-            last_c = jnp.where(q == 0, 7, jnp.where(q == 1, 6, jnp.where(q == 2, 5, 7)))
-            ok = t >= 0
+            last_i = jnp.where(q == 3, 0, 2)
+            last_c = jnp.where(q == 3, 4, 5 + q)
         column = jnp.where(t < 8, own, jnp.where(t < 12, side, jnp.where(t < 36, own, side)))
         plane = jnp.where(t < 12, z, jnp.where(t < 36, plane_at(z, i), plane_at(z, last_i)))
         chunk = jnp.where(
-            t < 8, t, jnp.where(t < 12, 2 * (t - 8) + way, jnp.where(t < 36, (t - 12) % 8, last_c))
-        )
+            t < 8, t, jnp.where(t < 12, 2 * (t - 8) + way, jnp.where(t < 36, turned(t - 12), last_c))
+        )
+        ends = jnp.logical_or(z == 0, z == 3)
+        ok = t >= 0 if way == X else jnp.logical_or(t != 39, ends)
         return column, plane, chunk, ok
+    extra = jnp.logical_and(t == 30, z == (0 if way == UP else 3))
     far = jnp.where(t < 24, t // 8, jnp.where(t < 30, 0, jnp.where(t < 35, 1, 2)))
-    chunk = jnp.where(t < 24, t % 8, jnp.where(t < 30, t - 24, jnp.where(t < 35, t - 30, t - 35)))
+    far = jnp.where(extra, 0, far)
+    k = jnp.where(t < 30, t - 24, (t - 30) % 5)
     column = jnp.where(t < 24, own, diagonal)
     if way == UP:
         plane = z - far
         ok = jnp.logical_and(jnp.logical_and(z >= 0, z < 3), plane >= 0)
+        i = jnp.where(z == 1, far + 1, far)
     else:
         plane = z + far
         ok = jnp.logical_and(jnp.logical_and(z <= 3, z > 0), plane <= 3)
+        i = jnp.where(z == 2, far + 1, far)
+    fifth = jnp.where(i == 2, 4, 5)
+    chunk = jnp.where(t < 24, t % 8, jnp.where(k < 4, k, jnp.where(k == 4, fifth, 6)))
+    chunk = jnp.where(extra, 4, chunk)
+    ok = jnp.logical_and(ok, jnp.logical_or(t != 29, i == 0))
     return column, plane, chunk, ok
 
 
 def units_ready(s):
     early = jnp.clip(s - 15, 0, 8) + 2 * jnp.clip(s - 27, 0, 8)
-    late = jnp.clip(s - 34, 0, 4) + jnp.where(s >= 38, 1, 0) + jnp.where(s >= 39, 3, 0)
+    late = jnp.clip(s - 34, 0, 1) + 2 * jnp.clip(s - 35, 0, 3)
     return early + late
 
 
@@ -81,14 +93,13 @@
         return held.at[chunk, pl.ds(start, rows), :]
 
     load_amps = pltpu.make_async_copy(tamps_hbm, amps, amps_sem)
-    loads = [
-        pltpu.make_async_copy(
-            slab_hbm.at[:, pl.ds(c * wide, wide)], place(own, z, c), own_sem.at[c]
-        )
-        for c in range(CHUNKS)
-    ]
-    for load in loads:
-        load.start()
+
+    def load(c):
+        cut = pl.ds(pl.multiple_of(c * wide, wide), wide)
+        return pltpu.make_async_copy(slab_hbm.at[:, cut], place(own, z, c), own_sem.at[c])
+
+    for c in range(CHUNKS):
+        load(c).start()
 
     barrier = pltpu.get_barrier_semaphore()
     side = (device(1 - x, y, z), device(x, 1 - y, z))
@@ -106,9 +117,6 @@
 
     ends = jnp.logical_or(z == 0, z == 3)
     pl.semaphore_wait(barrier, jnp.where(ends, 4, 5))
-
-    for load in loads:
-        load.wait()
 
     targets = (side[0], side[1], me + 4, me - 4)
     sources = ((1 - x, y, z), (x, 1 - y, z), (x, y, z - 1), (x, y, z + 1))
@@ -138,6 +146,14 @@
             @pl.when(ok)
             def _():
                 copy(way, t, place(column, plane, chunk)).wait_recv()
+
+    def sent(t):
+        for way in range(4):
+            column, plane, chunk, ok = message(way, t, x, y, z)
+
+            @pl.when(ok)
+            def _():
+                copy(way, t, place(column, plane, chunk)).wait_send()
 
     def product(u):
         m = u - 24
@@ -151,13 +167,18 @@
                 (1 - y) * 2 + 1 - x,
             ),
         )
-        late = jnp.where(m == 4, 5, jnp.where(m == 5, 4, m))
-        chunk = jnp.where(u < 8, u, jnp.where(u < 24, pair // 2, late))
-        left = held[chunk, pl.ds(pl.multiple_of(column * 4 * rows, 4 * rows), 4 * rows), :]
+        late = jnp.where(m % 2 == 1, (m + 1) // 2, jnp.where(m == 0, 0, 4 + m // 2))
+        chunk = jnp.where(u < 8, u, jnp.where(u < 24, (pair // 2 + 5) % 8, late))
+        multiply(column, chunk, 0, 4 * rows)
+
+    def multiply(column, chunk, first_row, count):
+        start = pl.multiple_of(column * 4 * rows + first_row, count)
+        left = held[chunk, pl.ds(start, count), :]
         deep = pl.ds(pl.multiple_of(chunk * wide, wide), wide)
+        into = pl.ds(pl.multiple_of(first_row, count), count)
         for first in range(0, columns, 256):
             cut = slice(first, min(first + 256, columns))
-            total[column, :, cut] += jnp.dot(
+            total[column, into, cut] += jnp.dot(
                 left, amps[deep, cut], preferred_element_type=jnp.float32
             )
 
@@ -171,52 +192,6 @@
             device_id_type=MESH,
         )
 
-    def step(t, _):
-        @pl.when(t >= LAG)
-        def _():
-            arrive(t - LAG)
-
-        @pl.when(t < SLOTS)
-        def _():
-            send(t)
-
-        @pl.when(t == 8)
-        def _():
-            load_amps.start()
-            total[...] = jnp.zeros_like(total)
-
-        @pl.when(t == 16)
-        def _():
-            load_amps.wait()
-
-        def unit(u, _):
-            product(u)
-            return 0
-
-        lax.fori_loop(units_ready(t - LAG - 1), units_ready(t - LAG), unit, 0)
-
-        @pl.when(t == 35 + LAG)
-        def _():
-            for column in (own, y * 2 + 1 - x, (1 - y) * 2 + x):
-                hand_over(column).start()
-
-        return 0
-
-    lax.fori_loop(0, SLOTS + LAG, step, 0)
-    hand_over((1 - y) * 2 + 1 - x).start()
-
-    def drain(t, _):
-        for way in range(4):
-            column, plane, chunk, ok = message(way, t, x, y, z)
-
-            @pl.when(ok)
-            def _():
-                copy(way, t, place(column, plane, chunk)).wait_send()
-
-        return 0
-
-    lax.fori_loop(0, SLOTS, drain, 0)
-
     def finish(column):
         hand_over(column).wait()
         mine = total[column, pl.ds(pl.multiple_of(core * half, half), half), :] + other[column]
@@ -224,8 +199,57 @@
             start = pl.multiple_of((k * 4 + column) * rows, rows)
             out_ref[pl.ds(start, rows), :] = mine[k * rows : (k + 1) * rows].astype(out_ref.dtype)
 
-    for column in (own, y * 2 + 1 - x, (1 - y) * 2 + x, (1 - y) * 2 + 1 - x):
-        finish(column)
+    def step(t, _):
+        @pl.when(t >= LAG)
+        def _():
+            arrive(t - LAG)
+
+        @pl.when(t < CHUNKS)
+        def _():
+            load(t).wait()
+
+        @pl.when(t < SLOTS)
+        def _():
+            send(t)
+
+        @pl.when(t >= LAG)
+        def _():
+            sent(t - LAG)
+
+        @pl.when(t == 8)
+        def _():
+            load_amps.start()
+            total[...] = jnp.zeros_like(total)
+
+        @pl.when(t == 16)
+        def _():
+            load_amps.wait()
+
+        def unit(u, _):
+            product(u)
+            return 0
+
+        lax.fori_loop(units_ready(t - LAG - 1), units_ready(t - LAG), unit, 0)
+
+        @pl.when(t == 35 + LAG)
+        def _():
+            for column in (own, y * 2 + 1 - x, (1 - y) * 2 + x):
+                hand_over(column).start()
+
+        @pl.when(t == SLOTS + LAG - 2)
+        def _():
+            for column in (own, y * 2 + 1 - x, (1 - y) * 2 + x):
+                finish(column)
+
+        return 0
+
+    lax.fori_loop(0, SLOTS + LAG, step, 0)
+    diagonal = (1 - y) * 2 + 1 - x
+    multiply(diagonal, 4, (1 - core) * half, half)
+    hand_over(diagonal).start()
+    multiply(diagonal, 4, core * half, half)
+
+    finish(diagonal)
 
 
 def linked(tamps, integrals):
@@ -233,7 +257,7 @@
     columns = tamps.shape[1]
     return pl.pallas_call(
         kernel,
-        out_shape=jax.ShapeDtypeStruct((8 * rows, columns), jnp.bfloat16),
+        out_shape=pltpu.VMEM((8 * rows, columns), jnp.bfloat16),
         in_specs=[pl.BlockSpec(memory_space=pl.ANY)] * 2,
         out_specs=pl.BlockSpec(memory_space=pltpu.VMEM),
         scratch_shapes=[

time: 128 us -> 123 us (0.961)
  Pallas kernels: 126 us -> 122 us
    pallas_call x1, Pallas kernels: 126 us -> 122 us  [linked(): pl.pallas_call(kernel, out_shape=pltpu.VMEM((8 * rows, columns), jnp.bflo...]
where the time goes in v2:
time: 123 us
  Pallas kernels  122 us (99%)
    pallas_call x1, Pallas kernels, linked(): pl.pallas_call(kernel, out_shape=pltpu.VMEM((8 * rows, columns), jnp.bflo...  122 us

profile of v2, /device:TPU:0, one launch (start us, length us, event | category | flops | bytes accessed | tf_op | source)
XLA Modules:
  0.0 123.3 jit_solution(5118475873450934059)
XLA Ops:
  0.0 122.4 %shard_map.28 = bf16[512,896]{1,0:T(8,128)(2,1)S(1)} custom-call(bf16[8192,896]{1,0:T(8,128)(2,1)} %tamps_hbm.1, bf16[64,8192]{1,0:T(8,128)(2,1)} %slab_hbm.1), custom_call_target="tpu_custom_call" | custom-call | tf_op jit(solution)/shard_map/pallas_call | solution.py:258
  122.4 0.9 copy.4

commit v3 on v2

--- a/solution.py
+++ b/solution.py
@@ -98,9 +98,6 @@
         cut = pl.ds(pl.multiple_of(c * wide, wide), wide)
         return pltpu.make_async_copy(slab_hbm.at[:, cut], place(own, z, c), own_sem.at[c])
 
-    for c in range(CHUNKS):
-        load(c).start()
-
     barrier = pltpu.get_barrier_semaphore()
     side = (device(1 - x, y, z), device(x, 1 - y, z))
     for to in side:
@@ -114,6 +111,9 @@
     @pl.when(z < 3)
     def _():
         pl.semaphore_signal(barrier, inc=1, device_id=(me + 4, core), device_id_type=MESH)
+
+    for c in range(CHUNKS):
+        load(c).start()
 
     ends = jnp.logical_or(z == 0, z == 3)
     pl.semaphore_wait(barrier, jnp.where(ends, 4, 5))
@@ -236,11 +236,6 @@
             for column in (own, y * 2 + 1 - x, (1 - y) * 2 + x):
                 hand_over(column).start()
 
-        @pl.when(t == SLOTS + LAG - 2)
-        def _():
-            for column in (own, y * 2 + 1 - x, (1 - y) * 2 + x):
-                finish(column)
-
         return 0
 
     lax.fori_loop(0, SLOTS + LAG, step, 0)
@@ -249,7 +244,8 @@
     hand_over(diagonal).start()
     multiply(diagonal, 4, core * half, half)
 
-    finish(diagonal)
+    for column in (own, y * 2 + 1 - x, (1 - y) * 2 + x, diagonal):
+        finish(column)
 
 
 def linked(tamps, integrals):

time: 123 us -> 123 us (level)
  no operation moved by 1% of the time
where the time goes in v3:
time: 123 us
  Pallas kernels  122 us (99%)
    pallas_call x1, Pallas kernels, linked(): pl.pallas_call(kernel, out_shape=pltpu.VMEM((8 * rows, columns), jnp.bflo...  122 us

profile of v3, /device:TPU:0, one launch (start us, length us, event | category | flops | bytes accessed | tf_op | source)
XLA Modules:
  0.0 123.2 jit_solution(8858661631793974692)
XLA Ops:
  0.0 122.3 %shard_map.28 = bf16[512,896]{1,0:T(8,128)(2,1)S(1)} custom-call(bf16[8192,896]{1,0:T(8,128)(2,1)} %tamps_hbm.1, bf16[64,8192]{1,0:T(8,128)(2,1)} %slab_hbm.1), custom_call_target="tpu_custom_call" | custom-call | tf_op jit(solution)/shard_map/pallas_call | solution.py:254
  122.3 0.9 copy.4

commit v4 on v3

--- a/solution.py
+++ b/solution.py
@@ -132,7 +132,7 @@
         )
 
     def send(t):
-        for way in range(4):
+        for way in (UP, DOWN, X, Y):
             column, plane, chunk, ok = message(way, t, x, y, z)
 
             @pl.when(ok)
@@ -140,7 +140,7 @@
                 copy(way, t, place(column, plane, chunk)).start()
 
     def arrive(t):
-        for way in range(4):
+        for way in (UP, DOWN, X, Y):
             column, plane, chunk, ok = message(way, t, *sources[way])
 
             @pl.when(ok)
@@ -148,7 +148,7 @@
                 copy(way, t, place(column, plane, chunk)).wait_recv()
 
     def sent(t):
-        for way in range(4):
+        for way in (UP, DOWN, X, Y):
             column, plane, chunk, ok = message(way, t, x, y, z)
 
             @pl.when(ok)

time: 123 us -> 123 us (level)
  no operation moved by 1% of the time
where the time goes in v4:
time: 123 us
  Pallas kernels  122 us (99%)
    pallas_call x1, Pallas kernels, linked(): pl.pallas_call(kernel, out_shape=pltpu.VMEM((8 * rows, columns), jnp.bflo...  122 us

profile of v4, /device:TPU:0, one launch (start us, length us, event | category | flops | bytes accessed | tf_op | source)
XLA Modules:
  0.0 123.2 jit_solution(18364113999855656465)
XLA Ops:
  0.0 122.3 %shard_map.28 = bf16[512,896]{1,0:T(8,128)(2,1)S(1)} custom-call(bf16[8192,896]{1,0:T(8,128)(2,1)} %tamps_hbm.1, bf16[64,8192]{1,0:T(8,128)(2,1)} %slab_hbm.1), custom_call_target="tpu_custom_call" | custom-call | tf_op jit(solution)/shard_map/pallas_call | solution.py:254
  122.3 0.9 copy.4
